TPU v7x, 256 devices: a whole 4x4x8 slice. The times are simulated.
256 devices in a mesh: tm: 32 (over x, z), chan: 8 (over y, core).
Axes of the slice: x: 4, y: 4, z: 8, core: 2. Of those that a mesh axis runs over, the one named last changes fastest.
Arguments:
- visibilities: bfloat16 [32, 8, 512, 1024], P('tm', None, None, 'chan'), may hold values from -6 to 6
- station_gains: float32 [8, 192, 1024], P(None, 'chan'), may hold values from -1.5 to 1.5, as said below
- station_pairs: int32 [512, 2], replicated, may hold values from 0 to 191, as said below
- average_bands: int32 [512, 2], replicated, may hold values from 0 to 3, as said below
- tile_map: int32 [512, 32], replicated, may hold values from 0 to 255
- baseline_order: int32 [512], replicated, may hold values from 0 to 511, as said below
Outputs:
- averaged: bfloat16 [32, 8, 512, 1024], P(None, None, 'tm', 'chan')
- gridded: float32 [256, 8, 1024], P('tm', None, 'chan')
Inputs may be any that keep to these rules, and one draw needn't show every extreme that they name: `station_pairs`: row b holds the two stations of baseline b, the first smaller than the second. `average_bands`: column 0 is at most 3, column 1 at most 2. In each aligned block of 16 positions k of baseline_order, the bands of the baselines baseline_order[k] are, in some order, the pairs (3 - j % (3 + 1), 2 - j % (2 + 1)) for j = 0 to 15. `baseline_order`: each baseline once. `station_gains`: diagonal Jones entries have magnitudes of order one.
All inputs are finite; a program needn't handle non-finite values.
Results may differ from a plain program's by a relative error of at most 0.019.
Values may be sent and summed in bfloat16 or wider, within the bound.
No kernel may reach another device: no remote copies, remote signals or barrier semaphores. Data moves between devices by JAX's collectives and lax.ppermute only.
A program may use at most 128 MiB of HBM per device.

v0:
```python
import jax
import jax.numpy as jnp
from jax import lax
from jax.sharding import PartitionSpec as P

TILE_DEV = 8
TLOG = 3
CLOG = 2


def product(left, right):
    return (left[0] * right[0] - left[1] * right[1], left[0] * right[1] + left[1] * right[0])


def product_conj(left, right):
    return (left[0] * right[0] + left[1] * right[1], left[1] * right[0] - left[0] * right[1])


def add_pair(left, right):
    return (left[0] + right[0], left[1] + right[1])


def as_matrix(components):
    return [
        [(components[0], components[1]), (components[2], components[3])],
        [(components[4], components[5]), (components[6], components[7])],
    ]


def jones_apply(first, middle, second):
    left_gain = as_matrix(first)
    coherency = as_matrix(middle)
    right_gain = as_matrix(second)
    partial_rows = [
        [
            add_pair(
                product(left_gain[i][0], coherency[0][k]), product(left_gain[i][1], coherency[1][k])
            )
            for k in range(2)
        ]
        for i in range(2)
    ]
    result = []
    for i in range(2):
        for c in range(2):
            element = add_pair(
                product_conj(partial_rows[i][0], right_gain[c][0]),
                product_conj(partial_rows[i][1], right_gain[c][1]),
            )
            result.extend(element)
    return result


def calibrate(samples, gain_table, first_station, second_station):
    left_gain = jnp.take(gain_table, first_station, axis=1)
    right_gain = jnp.take(gain_table, second_station, axis=1)
    values = [samples[:, i].astype(jnp.float32) for i in range(8)]
    result = jones_apply(
        [left_gain[i][None] for i in range(8)], values, [right_gain[i][None] for i in range(8)]
    )
    return jnp.stack(result, axis=1).astype(jnp.bfloat16)


def halve_time(current, size):
    extent = current.shape[0]
    shaped = current.reshape((extent // size, 2, size // 2) + current.shape[1:])
    merged = 0.5 * (shaped[:, 0:1] + shaped[:, 1:2])
    return jnp.broadcast_to(merged, shaped.shape).reshape(current.shape)


def halve_chan(current, size):
    extent = current.shape[-1]
    shaped = current.reshape(current.shape[:-1] + (extent // size, 2, size // 2))
    merged = 0.5 * (shaped[..., 0:1, :] + shaped[..., 1:2, :])
    return jnp.broadcast_to(merged, shaped.shape).reshape(current.shape)


def band_average(samples, time_levels, chan_levels):
    values = samples.astype(jnp.float32)
    time_select = time_levels[None, None, :, None]
    chan_select = chan_levels[None, None, :, None]
    result = values
    current = values
    for k in range(1, TLOG + 1):
        current = halve_time(current, 2**k)
        result = jnp.where(time_select >= k, current, result)
    final = result
    current = result
    for k in range(1, CLOG + 1):
        current = halve_chan(current, 2**k)
        final = jnp.where(chan_select >= k, current, final)
    return final.astype(jnp.bfloat16)


def shards(visibilities, station_gains, station_pairs, average_bands, tile_map, baseline_order):
    chan_width = visibilities.shape[3]
    block_size = visibilities.shape[2] // lax.axis_size("tm")
    all_gains = lax.all_gather(station_gains, "chan", axis=1, tiled=True)
    gain_table = lax.dynamic_slice_in_dim(
        all_gains, lax.axis_index("chan") * chan_width, chan_width, 2
    )
    reordered = jnp.take(visibilities, baseline_order, axis=2)
    rows_here = lax.dynamic_slice_in_dim(
        baseline_order, lax.axis_index("tm") * block_size, block_size
    )
    bands_here = average_bands[rows_here]
    ordered_pairs = station_pairs[baseline_order]
    payload = calibrate(reordered, gain_table, ordered_pairs[:, 0], ordered_pairs[:, 1])
    turned = lax.all_to_all(payload, "tm", split_axis=2, concat_axis=0, tiled=True)
    averaged = band_average(turned, bands_here[:, 0], bands_here[:, 1])
    tile_here = tile_map[rows_here].T
    time_index = jnp.arange(averaged.shape[0], dtype=jnp.int32)[:, None]
    period = jnp.left_shift(jnp.ones_like(bands_here[:, 0]), bands_here[:, 0])[None, :]
    tile_ids = jnp.where(time_index % period == 0, tile_here, -1)
    targets = jnp.arange(TILE_DEV * lax.axis_size("tm"), dtype=jnp.int32)
    one_hot = (tile_ids[None] == targets[:, None, None]).astype(jnp.bfloat16)
    gridded = lax.psum_scatter(
        jnp.einsum("rtb,tkbc->rkc", one_hot, averaged, preferred_element_type=jnp.float32).astype(
            jnp.bfloat16
        ),
        "tm",
        scatter_dimension=0,
        tiled=True,
    ).astype(jnp.float32)
    return (averaged, gridded)


def solution(mesh):
    return jax.shard_map(
        shards,
        mesh=mesh,
        in_specs=(P("tm", None, None, "chan"), P(None, "chan", None), P(), P(), P(), P()),
        out_specs=(P(None, None, "tm", "chan"), P("tm", None, "chan")),
        check_vma=False,
    )
```

profile of v0, /device:TPU:8, one launch (start us, length us, event | category | flops | bytes accessed | tf_op | source)
XLA Modules:
  0.0 475.1 jit_solution(13990417689148985308)
XLA Ops:
  14.1 41.8 %all-gather.2.cloned.1.call-done = f32[8,192,1024]{2,0,1:T(8,128)} async-done(((f32[8,24,1024]{2,0,1:T(8,128)}), f32[8,192,1024]{2,0,1:T(8,128)}) %all-gather.2.cloned.1.call-update) | async-done | bytes 6291472 | tf_op jit(solution)/shard_map/all_gather | solution.py:98
  57.1 2.7 gather_fusion.5
  59.8 2.7 gather_fusion.4
  68.5 9.8 %all-to-all-start = ((bf16[1,8,512,128]{3,1,0,2:T(8,128)(2,1)}), bf16[1,8,512,128]{3,1,0,2:T(8,128)(2,1)S(1)}, u32[]{:S(2)}, u32[]{:S(2)}) async-start(bf16[1,8,512,128]{3,1,0,2:T(8,128)(2,1)} %copy.591), calls=%async_computation | async-start | bytes 2097152 | tf_op jit(solution)/shard_map/all_to_all | solution.py:109
  81.0 26.3 %all-to-all-done = bf16[1,8,512,128]{3,1,0,2:T(8,128)(2,1)S(1)} async-done(((bf16[1,8,512,128]{3,1,0,2:T(8,128)(2,1)}), bf16[1,8,512,128]{3,1,0,2:T(8,128)(2,1)S(1)}, u32[]{:S(2)}, u32[]{:S(2)}) %all-to-all-start) | async-done | bytes 1048608 | tf_op jit(solution)/shard_map/all_to_all | solution.py:109
  110.6 2.8 copy.621
  116.0 5.8 %add_multiply_fusion = f32[8,1,8,16,128]{3,2,4,0,1:T(8,128)} fusion(f32[8,1,8,16,128]{3,2,4,0,1:T(8,128)} %copy.620, f32[8,1,8,16,128]{3,2,4,0,1:T(8,128)} %copy.621), kind=kLoop, calls=%fused_computation.7 | loop fusion | flops 262144 | bytes 1572864 | tf_op jit(solution)/shard_map/mul | solution.py:67
  121.8 2.7 copy.625
  127.6 6.6 %copy.598 = f32[32,1,8,16,128]{0,3,4,2,1:T(8,128)} copy(f32[32,1,8,16,128]{4,3,0,2,1:T(8,128)} %convert_bitcast_fusion) | data formatting | bytes 4194304 | tf_op jit(solution)/shard_map/convert_element_type | solution.py:79
  134.2 8.7 %copy.600 = f32[32,8,16,64,2,1]{3,2,5,4,1,0:T(8,128)} copy(f32[32,8,16,64,2,1]{0,2,4,3,1,5:T(8,128)} %bitcast.225) | data formatting | bytes 4194304 | tf_op jit(solution)/shard_map/convert_element_type | solution.py:79
  142.9 6.0 %copy.597 = f32[16,8,16,128]{2,1,3,0:T(8,128)} copy(f32[16,8,16,128]{3,2,0,1:T(8,128)} %fusion.59) | data formatting | bytes 2097152 | tf_op jit(solution)/shard_map/broadcast_in_dim | solution.py:68
  148.9 11.0 %broadcast_in_dim.122 = f32[16,2,8,16,128]{3,2,4,1,0:T(8,128)} broadcast(f32[16,8,16,128]{2,1,3,0:T(8,128)} %copy.597), dimensions={0,2,3,4} | broadcast | bytes 3145728 | tf_op jit(solution)/shard_map/broadcast_in_dim | solution.py:68
  159.9 11.9 %copy.599 = f32[32,8,16,64,2,1]{3,2,5,4,1,0:T(8,128)} copy(f32[32,8,16,64,2,1]{2,1,4,3,0,5:T(8,128)} %bitcast.219) | data formatting | bytes 4194304 | tf_op jit(solution)/shard_map/broadcast_in_dim | solution.py:68
  171.8 7.6 %broadcast_in_dim.117 = f32[4,2,4,8,16,128]{4,3,5,2,1,0:T(8,128)} broadcast(f32[4,8,16,128]{2,1,3,0:T(8,128)S(1)} %fusion.5), dimensions={0,3,4,5} | broadcast | bytes 2359296 | tf_op jit(solution)/shard_map/broadcast_in_dim | solution.py:68
  179.4 12.0 %copy.602 = f32[32,8,16,64,2,1]{3,2,5,4,1,0:T(8,128)} copy(f32[32,8,16,64,2,1]{2,1,4,3,0,5:T(8,128)} %bitcast.220) | data formatting | bytes 4194304 | tf_op jit(solution)/shard_map/reshape | solution.py:68
  191.4 10.2 %broadcast_in_dim.119 = f32[8,2,2,8,16,128]{4,3,5,2,1,0:T(8,128)} broadcast(f32[8,8,16,128]{2,1,3,0:T(8,128)} %bitcast.224), dimensions={0,3,4,5} | broadcast | bytes 2621440 | tf_op jit(solution)/shard_map/broadcast_in_dim | solution.py:68
  201.6 11.9 %copy.601 = f32[32,8,16,64,2,1]{3,2,5,4,1,0:T(8,128)} copy(f32[32,8,16,64,2,1]{2,1,4,3,0,5:T(8,128)} %bitcast.221) | data formatting | bytes 4194304 | tf_op jit(solution)/shard_map/reshape | solution.py:68
  213.5 8.0 %select_select_fusion = f32[32,8,16,64,2,1]{3,2,5,4,1,0:T(8,128)S(1)} fusion(f32[32,8,16,64,2,1]{3,2,5,4,1,0:T(8,128)} %copy.602, f32[32,8,16,64,2,1]{3,2,5,4,1,0:T(8,128)} %copy.601, f32[32,8,16,64,2,1]{3,2,5,4,1,0:T(8,128)} %copy.599, f32[32,8,16,64,2,1]{3,2,5,4,1,0:T(8,128)} %copy.600, pred[16]{0:T(512)(128)(4,1)S(1)} %get-tuple-element.31, ...), kind=kLoop, calls=%fused_computation.6 | loop fusion | flops 1572864 | bytes 10485808 | tf_op jit(solution)/shard_map/jit(_where)/select_n | solution.py:86
  223.6 4.5 copy.606
  228.2 4.1 broadcast_in_dim.128
  232.3 6.1 %copy.610 = bf16[32,8,16,128]{3,2,0,1:T(8,128)(2,1)} copy(bf16[32,8,16,128]{0,2,3,1:T(8,128)(2,1)} %bitcast.228) | data formatting | bytes 2097152 | tf_op jit(solution)/shard_map/broadcast_in_dim | solution.py:75
  238.4 3.6 copy.603
  247.0 6.2 %copy.611 = bf16[32,8,16,128]{3,2,0,1:T(8,128)(2,1)} copy(bf16[32,8,16,128]{0,2,3,1:T(8,128)(2,1)} %bitcast.230) | data formatting | bytes 2097152 | tf_op jit(solution)/shard_map/reshape | solution.py:75
  258.5 208.4 %reduce-scatter.4.cloned.1.call-done = bf16[8,1024]{1,0:T(8,128)(2,1)} async-done(((bf16[256,1024]{1,0:T(8,128)(2,1)}), bf16[8,1024]{1,0:T(8,128)(2,1)}) %reduce-scatter.4.cloned.1.call-update) | async-done | bytes 16400
  (89 shorter events, 39.1 us)
Async XLA Ops:
  7.2 2.7 copy-start.9
  7.2 2.8 copy-start.4
  7.2 3.5 copy-start.6
  7.2 48.7 %all-gather.2.cloned.1.call-start = ((), (), s32[]{:S(2)}) async-start(), calls=%async_computation.2 | async-start | bytes 7077888 | tf_op jit(solution)/shard_map/all_gather | solution.py:98
  62.5 2.2 copy-start.1
  66.8 11.6 %copy-start.10 = (s32[512,2]{0,1:T(2,128)S(1)}, s32[512,2]{0,1:T(2,128)}, u32[]{:S(2)}) copy-start(s32[512,2]{0,1:T(2,128)} %param.11) | copy-start | bytes 12292
  66.8 11.7 %copy-start.5 = (s32[512,32]{0,1:T(8,128)S(1)}, s32[512,32]{0,1:T(8,128)}, u32[]{:S(2)}) copy-start(s32[512,32]{0,1:T(8,128)} %param.12) | copy-start | bytes 196612
  68.5 38.8 %all-to-all-start = ((bf16[1,8,512,128]{3,1,0,2:T(8,128)(2,1)}), bf16[1,8,512,128]{3,1,0,2:T(8,128)(2,1)S(1)}, u32[]{:S(2)}, u32[]{:S(2)}) async-start(bf16[1,8,512,128]{3,1,0,2:T(8,128)(2,1)} %copy.591), calls=%async_computation | async-start | bytes 2097152 | tf_op jit(solution)/shard_map/all_to_all | solution.py:109
  78.3 388.6 %reduce-scatter.4.cloned.1.call-start = ((), (), s32[]{:S(2)}) async-start(), calls=%async_computation.3 | async-start | bytes 540672
  201.6 11.9 %copy-start.7 = (pred[16]{0:T(512)(128)(4,1)S(1)}, pred[16]{0:T(512)(128)(4,1)}, u32[]{:S(2)}) copy-start(pred[16]{0:T(512)(128)(4,1)} %get-tuple-element.33) | copy-start | bytes 52
  247.0 6.2 %copy-start = (f32[16,8,16,128]{3,2,0,1:T(8,128)S(1)}, f32[16,8,16,128]{3,2,0,1:T(8,128)}, u32[]{:S(2)}) copy-start(f32[16,8,16,128]{3,2,0,1:T(8,128)} %fusion.59) | copy-start | bytes 3145732
  253.2 1.2 copy-start.2
  253.2 1.5 copy-start.3
  253.2 1.5 copy-start.8
  253.2 1.5 copy-start.11
  253.2 1.5 copy-start.12
Sparse Core Ops, SparseCore 0:
  10.4 45.4 all-gather.1
  257.4 209.4 reduce-scatter.3
where the time goes:
time: 476 us; the launch traced here: 475 us
  waiting for transfers between devices  276 us (58%)
  local copies, waits for them, and re-layouts  142 us (30%)
  other arithmetic  31.2 us (7%)
  between operations  14.4 us (3%)
  starting transfers between devices  9.9 us (2%)
    unnamed x3, waiting for transfers between devices  208 us
    broadcast_in_dim x8, local copies, waits for them, and re-layouts, halve_time(): return jnp.broadcast_to(merged, shaped.shape).reshape(current.shape)  47.1 us
    all_gather x1, waiting for transfers between devices, shards(): all_gains = lax.all_gather(station_gains, 'chan', axis=1, tiled=True)  41.8 us
    all_to_all x1, waiting for transfers between devices, shards(): lax.all_to_all(payload, 'tm', split_axis=2, concat_axis=0, tiled=True)  26.3 us
    reshape x2, local copies, waits for them, and re-layouts, halve_time(): return jnp.broadcast_to(merged, shaped.shape).reshape(current.shape)  23.9 us
    broadcast_in_dim x4, local copies, waits for them, and re-layouts, halve_chan(): return jnp.broadcast_to(merged, shaped.shape).reshape(current.shape)  17.2 us
    unnamed x38, local copies, waits for them, and re-layouts  16.4 us
    convert_element_type x2, local copies, waits for them, and re-layouts, band_average(): values = samples.astype(jnp.float32)  15.3 us
  transfers between devices with their start and end apart: 3, of which 3 were waited for; matrix products, arithmetic and copies ran while one was open for 2% of the time, Pallas kernels for 0%

commit v1 on v0

--- a/solution.py
+++ b/solution.py
@@ -95,7 +95,9 @@
 def shards(visibilities, station_gains, station_pairs, average_bands, tile_map, baseline_order):
     chan_width = visibilities.shape[3]
     block_size = visibilities.shape[2] // lax.axis_size("tm")
-    all_gains = lax.all_gather(station_gains, "chan", axis=1, tiled=True)
+    all_gains = jnp.concatenate(
+        lax.all_to_all(jnp.stack([station_gains] * lax.axis_size("chan")), "chan", 0, 0), axis=1
+    )
     gain_table = lax.dynamic_slice_in_dim(
         all_gains, lax.axis_index("chan") * chan_width, chan_width, 2
     )

time: 476 us -> 511 us (1.074)
  waiting for transfers between devices: 276 us -> 300 us
  starting transfers between devices: 9.9 us -> 16.6 us
    all_to_all x0 -> x1, waiting for transfers between devices: none -> 66.5 us  [shards(): lax.all_to_all(jnp.stack([station_gains] * lax.axis_size('chan')), 'chan'...]
    all_gather x1 -> x0, waiting for transfers between devices: 41.8 us -> none  [shards(): all_gains = lax.all_gather(station_gains, 'chan', axis=1, tiled=True)]
    all_to_all x0 -> x1, starting transfers between devices: none -> 6.95 us  [shards(): lax.all_to_all(jnp.stack([station_gains] * lax.axis_size('chan')), 'chan'...]
    unnamed x3 -> x2, waiting for transfers between devices: 208 us -> 208 us
where the time goes in v1:
time: 511 us; the launch traced here: 510 us
  waiting for transfers between devices  300 us (59%)
  local copies, waits for them, and re-layouts  147 us (29%)
  other arithmetic  31.2 us (6%)
  starting transfers between devices  16.6 us (3%)
  between operations  14.4 us (3%)
    unnamed x2, waiting for transfers between devices  208 us
    all_to_all x1, waiting for transfers between devices, shards(): lax.all_to_all(jnp.stack([station_gains] * lax.axis_size('chan')), 'chan'...  66.5 us
    broadcast_in_dim x8, local copies, waits for them, and re-layouts, halve_time(): return jnp.broadcast_to(merged, shaped.shape).reshape(current.shape)  47.1 us
    all_to_all x1, waiting for transfers between devices, shards(): lax.all_to_all(payload, 'tm', split_axis=2, concat_axis=0, tiled=True)  25.8 us
    reshape x2, local copies, waits for them, and re-layouts, halve_time(): return jnp.broadcast_to(merged, shaped.shape).reshape(current.shape)  23.9 us
    broadcast_in_dim x4, local copies, waits for them, and re-layouts, halve_chan(): return jnp.broadcast_to(merged, shaped.shape).reshape(current.shape)  17.2 us
    convert_element_type x2, local copies, waits for them, and re-layouts, band_average(): values = samples.astype(jnp.float32)  15.4 us
    unnamed x38, local copies, waits for them, and re-layouts  14.3 us
  transfers between devices with their start and end apart: 3, of which 3 were waited for; matrix products, arithmetic and copies ran while one was open for 2% of the time, Pallas kernels for 0%

profile of v1, /device:TPU:8, one launch (start us, length us, event | category | flops | bytes accessed | tf_op | source)
XLA Modules:
  0.0 510.2 jit_solution(7312626645357967211)
XLA Ops:
  7.2 4.6 stack.38
  11.8 6.9 %all-to-all-start = ((f32[8,8,24,1024]{3,2,1,0:T(8,128)}), f32[8,8,24,1024]{3,2,1,0:T(8,128)}, u32[]{:S(2)}, u32[]{:S(2)}) async-start(f32[8,8,24,1024]{3,2,1,0:T(8,128)} %stack.38), calls=%async_computation | async-start | bytes 12582912 | tf_op jit(solution)/shard_map/all_to_all | solution.py:99
  23.0 66.5 %all-to-all-done = f32[8,8,24,1024]{3,2,1,0:T(8,128)} async-done(((f32[8,8,24,1024]{3,2,1,0:T(8,128)}), f32[8,8,24,1024]{3,2,1,0:T(8,128)}, u32[]{:S(2)}, u32[]{:S(2)}) %all-to-all-start) | async-done | bytes 6291488 | tf_op jit(solution)/shard_map/all_to_all | solution.py:99
  89.5 3.4 copy.587
  104.9 9.6 %all-to-all-start.1 = ((bf16[1,8,512,128]{3,1,0,2:T(8,128)(2,1)}), bf16[1,8,512,128]{3,1,0,2:T(8,128)(2,1)S(1)}, u32[]{:S(2)}, u32[]{:S(2)}) async-start(bf16[1,8,512,128]{3,1,0,2:T(8,128)(2,1)} %copy.593), calls=%async_computation.1 | async-start | bytes 2097152 | tf_op jit(solution)/shard_map/all_to_all | solution.py:111
  117.2 25.8 %all-to-all-done.1 = bf16[1,8,512,128]{3,1,0,2:T(8,128)(2,1)S(1)} async-done(((bf16[1,8,512,128]{3,1,0,2:T(8,128)(2,1)}), bf16[1,8,512,128]{3,1,0,2:T(8,128)(2,1)S(1)}, u32[]{:S(2)}, u32[]{:S(2)}) %all-to-all-start.1) | async-done | bytes 1048608 | tf_op jit(solution)/shard_map/all_to_all | solution.py:111
  146.3 2.8 copy.624
  151.7 5.8 %add_multiply_fusion = f32[8,1,8,16,128]{3,2,4,0,1:T(8,128)} fusion(f32[8,1,8,16,128]{3,2,4,0,1:T(8,128)} %copy.623, f32[8,1,8,16,128]{3,2,4,0,1:T(8,128)} %copy.624), kind=kLoop, calls=%fused_computation.7 | loop fusion | flops 262144 | bytes 1572864 | tf_op jit(solution)/shard_map/mul | solution.py:67
  163.3 6.6 %copy.600 = f32[32,1,8,16,128]{0,3,4,2,1:T(8,128)} copy(f32[32,1,8,16,128]{4,3,0,2,1:T(8,128)} %convert_bitcast_fusion) | data formatting | bytes 4194304 | tf_op jit(solution)/shard_map/convert_element_type | solution.py:79
  169.9 8.8 %copy.602 = f32[32,8,16,64,2,1]{3,2,5,4,1,0:T(8,128)} copy(f32[32,8,16,64,2,1]{0,2,4,3,1,5:T(8,128)} %bitcast.228) | data formatting | bytes 4194304 | tf_op jit(solution)/shard_map/convert_element_type | solution.py:79
  178.7 6.0 %copy.599 = f32[16,8,16,128]{2,1,3,0:T(8,128)} copy(f32[16,8,16,128]{3,2,0,1:T(8,128)} %fusion.59) | data formatting | bytes 2097152 | tf_op jit(solution)/shard_map/broadcast_in_dim | solution.py:68
  184.6 11.0 %broadcast_in_dim.122 = f32[16,2,8,16,128]{3,2,4,1,0:T(8,128)} broadcast(f32[16,8,16,128]{2,1,3,0:T(8,128)} %copy.599), dimensions={0,2,3,4} | broadcast | bytes 3145728 | tf_op jit(solution)/shard_map/broadcast_in_dim | solution.py:68
  195.6 12.0 %copy.601 = f32[32,8,16,64,2,1]{3,2,5,4,1,0:T(8,128)} copy(f32[32,8,16,64,2,1]{2,1,4,3,0,5:T(8,128)} %bitcast.222) | data formatting | bytes 4194304 | tf_op jit(solution)/shard_map/broadcast_in_dim | solution.py:68
  207.6 7.6 %broadcast_in_dim.117 = f32[4,2,4,8,16,128]{4,3,5,2,1,0:T(8,128)} broadcast(f32[4,8,16,128]{2,1,3,0:T(8,128)S(1)} %fusion.5), dimensions={0,3,4,5} | broadcast | bytes 2359296 | tf_op jit(solution)/shard_map/broadcast_in_dim | solution.py:68
  215.2 12.0 %copy.604 = f32[32,8,16,64,2,1]{3,2,5,4,1,0:T(8,128)} copy(f32[32,8,16,64,2,1]{2,1,4,3,0,5:T(8,128)} %bitcast.223) | data formatting | bytes 4194304 | tf_op jit(solution)/shard_map/reshape | solution.py:68
  227.1 10.2 %broadcast_in_dim.119 = f32[8,2,2,8,16,128]{4,3,5,2,1,0:T(8,128)} broadcast(f32[8,8,16,128]{2,1,3,0:T(8,128)} %bitcast.227), dimensions={0,3,4,5} | broadcast | bytes 2621440 | tf_op jit(solution)/shard_map/broadcast_in_dim | solution.py:68
  237.3 11.9 %copy.603 = f32[32,8,16,64,2,1]{3,2,5,4,1,0:T(8,128)} copy(f32[32,8,16,64,2,1]{2,1,4,3,0,5:T(8,128)} %bitcast.224) | data formatting | bytes 4194304 | tf_op jit(solution)/shard_map/reshape | solution.py:68
  249.2 8.0 %select_select_fusion = f32[32,8,16,64,2,1]{3,2,5,4,1,0:T(8,128)S(1)} fusion(f32[32,8,16,64,2,1]{3,2,5,4,1,0:T(8,128)} %copy.604, f32[32,8,16,64,2,1]{3,2,5,4,1,0:T(8,128)} %copy.603, f32[32,8,16,64,2,1]{3,2,5,4,1,0:T(8,128)} %copy.601, f32[32,8,16,64,2,1]{3,2,5,4,1,0:T(8,128)} %copy.602, pred[16]{0:T(512)(128)(4,1)S(1)} %get-tuple-element.31, ...), kind=kLoop, calls=%fused_computation.6 | loop fusion | flops 1572864 | bytes 10485808 | tf_op jit(solution)/shard_map/jit(_where)/select_n | solution.py:86
  259.4 4.5 copy.608
  263.9 4.1 broadcast_in_dim.128
  268.0 6.1 %copy.612 = bf16[32,8,16,128]{3,2,0,1:T(8,128)(2,1)} copy(bf16[32,8,16,128]{0,2,3,1:T(8,128)(2,1)} %bitcast.231) | data formatting | bytes 2097152 | tf_op jit(solution)/shard_map/broadcast_in_dim | solution.py:75
  274.1 3.6 copy.605
  282.8 6.2 %copy.613 = bf16[32,8,16,128]{3,2,0,1:T(8,128)(2,1)} copy(bf16[32,8,16,128]{0,2,3,1:T(8,128)(2,1)} %bitcast.233) | data formatting | bytes 2097152 | tf_op jit(solution)/shard_map/reshape | solution.py:75
  294.3 207.7 %reduce-scatter.4.cloned.1.call-done = bf16[8,1024]{1,0:T(8,128)(2,1)} async-done(((bf16[256,1024]{1,0:T(8,128)(2,1)}), bf16[8,1024]{1,0:T(8,128)(2,1)}) %reduce-scatter.4.cloned.1.call-update) | async-done | bytes 16400
  (90 shorter events, 44.1 us)
Async XLA Ops:
  11.8 7.0 %copy-start.9 = (s32[512,2]{0,1:T(2,128)S(1)}, s32[512,2]{0,1:T(2,128)}, u32[]{:S(2)}) copy-start(s32[512,2]{0,1:T(2,128)} %param.10) | copy-start | bytes 12292
  11.8 7.1 %copy-start.4 = (bf16[1,8,512,128]{3,2,1,0:T(8,128)(2,1)S(1)}, bf16[1,8,512,128]{3,2,1,0:T(8,128)(2,1)}, u32[]{:S(2)}) copy-start(bf16[1,8,512,128]{3,2,1,0:T(8,128)(2,1)} %param.8) | copy-start | bytes 3145732
  11.8 77.8 %all-to-all-start = ((f32[8,8,24,1024]{3,2,1,0:T(8,128)}), f32[8,8,24,1024]{3,2,1,0:T(8,128)}, u32[]{:S(2)}, u32[]{:S(2)}) async-start(f32[8,8,24,1024]{3,2,1,0:T(8,128)} %stack.38), calls=%async_computation | async-start | bytes 12582912 | tf_op jit(solution)/shard_map/all_to_all | solution.py:99
  18.7 0.9 copy-start.6
  98.9 2.2 copy-start.1
  103.2 11.3 %copy-start.10 = (s32[512,2]{0,1:T(2,128)S(1)}, s32[512,2]{0,1:T(2,128)}, u32[]{:S(2)}) copy-start(s32[512,2]{0,1:T(2,128)} %param.11) | copy-start | bytes 12292
  103.2 11.5 %copy-start.5 = (s32[512,32]{0,1:T(8,128)S(1)}, s32[512,32]{0,1:T(8,128)}, u32[]{:S(2)}) copy-start(s32[512,32]{0,1:T(8,128)} %param.12) | copy-start | bytes 196612
  104.9 38.1 %all-to-all-start.1 = ((bf16[1,8,512,128]{3,1,0,2:T(8,128)(2,1)}), bf16[1,8,512,128]{3,1,0,2:T(8,128)(2,1)S(1)}, u32[]{:S(2)}, u32[]{:S(2)}) async-start(bf16[1,8,512,128]{3,1,0,2:T(8,128)(2,1)} %copy.593), calls=%async_computation.1 | async-start | bytes 2097152 | tf_op jit(solution)/shard_map/all_to_all | solution.py:111
  114.4 387.5 %reduce-scatter.4.cloned.1.call-start = ((), (), s32[]{:S(2)}) async-start(), calls=%async_computation.3 | async-start | bytes 540672
  237.3 11.9 %copy-start.7 = (pred[16]{0:T(512)(128)(4,1)S(1)}, pred[16]{0:T(512)(128)(4,1)}, u32[]{:S(2)}) copy-start(pred[16]{0:T(512)(128)(4,1)} %get-tuple-element.33) | copy-start | bytes 52
  282.8 6.2 %copy-start = (f32[16,8,16,128]{3,2,0,1:T(8,128)S(1)}, f32[16,8,16,128]{3,2,0,1:T(8,128)}, u32[]{:S(2)}) copy-start(f32[16,8,16,128]{3,2,0,1:T(8,128)} %fusion.59) | copy-start | bytes 3145732
  289.0 1.2 copy-start.2
  289.0 1.5 copy-start.3
  289.0 1.5 copy-start.8
  289.0 1.5 copy-start.11
  289.0 1.5 copy-start.12
Sparse Core Ops, SparseCore 0:
  293.2 208.7 reduce-scatter.3
